TPU v7x, 1024 devices: a whole 8x8x8 slice. The times are simulated.
1024 devices in a mesh: ctx: 128 (over z, x, core), head: 8 (over y).
Axes of the slice: x: 8, y: 8, z: 8, core: 2. Of those that a mesh axis runs over, the one named last changes fastest.
Arguments:
- queries: bfloat16 [32768, 16, 128], P('ctx', 'head'), may hold values from -6 to 6
- spikes: int32 [32768, 16, 128], P('ctx', 'head'), may hold values from 0 to 3
- values: bfloat16 [32768, 16, 128], P('ctx', 'head'), may hold values from -6 to 6
- threshold: float32 [128], replicated, may hold values from 0.05 to 0.5
- norm_gain: float32 [128], replicated, may hold values from 0.1 to 1.9
- document_ids: int32 [32768], P('ctx'), may hold values from 0 to 511, never falling along the last dimension, each value on 1 to 8192 neighbouring positions
- cotangent: bfloat16 [32768, 16, 128], P('ctx', 'head'), may hold values from -6 to 6
Outputs:
- attended: bfloat16 [32768, 16, 128], P('ctx', 'head')
- query_grad: bfloat16 [32768, 16, 128], P('ctx', 'head')
- value_grad: bfloat16 [32768, 16, 128], P('ctx', 'head')
- threshold_grad: float32 [128], replicated
- gain_grad: float32 [128], replicated
Inputs may be any that keep to these rules, and one draw needn't show every extreme that they name: `document_ids`: ids never fall along the context; each document holds 1 to 8192 consecutive tokens, and one holds exactly 8192.
All inputs are finite; a program needn't handle non-finite values.
Results may differ from a plain program's by a relative error of at most 0.011.
Values sent between devices are 32-bit elements; how exact they have to be, the bound alone decides.
A program may use at most 128 MiB of HBM per device.

v0:
```python
import math

import jax
import jax.numpy as jnp
from jax import lax
from jax.sharding import PartitionSpec as P


def entering(value, axis, join, neutral, backward):
    count, mine = (lax.axis_size(axis), lax.axis_index(axis))
    pieces = jax.tree.map(lambda part: lax.all_gather(part, axis), value)
    if backward:
        pieces = jax.tree.map(lambda part: part[::-1], pieces)
        mine = count - 1 - mine
    so_far = jax.tree.map(
        lambda part, zero: jnp.full_like(part, 0) + jnp.asarray(zero, part.dtype), value, neutral
    )

    def step(position, so_far):
        longer = join(so_far, jax.tree.map(lambda part: part[position], pieces))
        return jax.tree.map(lambda new, old: jnp.where(position < mine, new, old), longer, so_far)

    return lax.fori_loop(0, count - 1, step, so_far)


def join_states(earlier, later):
    early_state, early_mark = earlier
    later_state, later_mark = later
    empty_later = later_mark < 0
    keeping = jnp.logical_or(early_mark == later_mark, empty_later).astype(jnp.float32)
    joined = later_state + keeping * early_state
    return (joined, jnp.where(empty_later, early_mark, later_mark))


def on_device(queries, spikes, values, threshold, norm_gain, document_ids, cotangent):
    length = queries.shape[0]
    head_count = queries.shape[1]
    width = queries.shape[2]
    keys_bf = (spikes.astype(jnp.float32) * threshold).astype(jnp.bfloat16)
    position = jnp.arange(length, dtype=jnp.int32)
    allowed = (position[None, :] <= position[:, None]) & (
        document_ids[:, None] == document_ids[None, :]
    )
    head_doc = document_ids[0]
    tail_doc = document_ids[-1]
    first_mask = document_ids == head_doc
    last_mask = document_ids == tail_doc
    first_bf = first_mask.astype(jnp.bfloat16)[:, None, None]
    last_bf = last_mask.astype(jnp.bfloat16)[:, None, None]
    first_f32 = first_mask.astype(jnp.float32)[:, None, None]
    last_f32 = last_mask.astype(jnp.float32)[:, None, None]
    zero_state = jnp.zeros((head_count, width, width), jnp.float32)
    identity = (zero_state, jnp.float32(-1.0))
    tail = jnp.einsum("thd,the->hde", keys_bf * last_bf, values, preferred_element_type=jnp.float32)
    before, before_mark = entering(
        (tail, tail_doc.astype(jnp.float32)), "ctx", join_states, identity, False
    )
    carried = jnp.where(before_mark == head_doc.astype(jnp.float32), before, 0.0).astype(
        jnp.bfloat16
    )
    raw_scores = jnp.einsum("shd,thd->hst", queries, keys_bf, preferred_element_type=jnp.float32)
    scores = jnp.where(allowed[None], raw_scores, 0.0).astype(jnp.bfloat16)
    inside = jnp.einsum("hst,thd->shd", scores, values, preferred_element_type=jnp.float32)
    mixed_raw = (
        queries.astype(jnp.float32)
        + inside
        + first_f32
        * jnp.einsum("shd,hde->she", queries, carried, preferred_element_type=jnp.float32)
    )
    ratio = lax.rsqrt(jnp.mean(mixed_raw * mixed_raw, axis=-1, keepdims=True) + 1e-06)
    normed = mixed_raw * ratio
    attended = (normed * norm_gain).astype(jnp.bfloat16)
    cot_f = cotangent.astype(jnp.float32)
    upstream = cot_f * norm_gain
    gnorm = (
        ratio * upstream - normed * ratio * jnp.mean(normed * upstream, axis=-1, keepdims=True)
    ).astype(jnp.bfloat16)
    gain_term = jnp.sum(cot_f * normed, axis=(0, 1))
    raw_dscores = jnp.einsum("shd,thd->hst", gnorm, values, preferred_element_type=jnp.float32)
    dscores = jnp.where(allowed[None], raw_dscores, 0.0).astype(jnp.bfloat16)
    tail_back = jnp.einsum(
        "shd,she->hde", queries * first_bf, gnorm, preferred_element_type=jnp.float32
    )
    after, after_mark = entering(
        (tail_back, head_doc.astype(jnp.float32)), "ctx", join_states, identity, True
    )
    returned = jnp.where(after_mark == tail_doc.astype(jnp.float32), after, 0.0).astype(
        jnp.bfloat16
    )
    query_grad = gnorm.astype(jnp.float32) + jnp.einsum(
        "hst,thd->shd", dscores, keys_bf, preferred_element_type=jnp.float32
    )
    query_grad = query_grad + first_f32 * jnp.einsum(
        "she,hde->shd", gnorm, carried, preferred_element_type=jnp.float32
    )
    key_grad = jnp.einsum("hst,shd->thd", dscores, queries, preferred_element_type=jnp.float32)
    key_grad = key_grad + last_f32 * jnp.einsum(
        "the,hde->thd", values, returned, preferred_element_type=jnp.float32
    )
    value_grad = jnp.einsum("hst,she->the", scores, gnorm, preferred_element_type=jnp.float32)
    value_grad = value_grad + last_f32 * jnp.einsum(
        "thd,hde->the", keys_bf, returned, preferred_element_type=jnp.float32
    )
    thresh_term = jnp.sum(spikes.astype(jnp.float32) * key_grad, axis=(0, 1))
    totals = lax.psum((thresh_term, gain_term), ("ctx", "head"))
    scale = 1.0 / math.sqrt(length * lax.axis_size("ctx") * head_count * lax.axis_size("head"))
    return (
        attended,
        query_grad.astype(jnp.bfloat16),
        value_grad.astype(jnp.bfloat16),
        totals[0] * scale,
        totals[1] * scale,
    )


def solution(mesh):
    placed = (
        P("ctx", "head", None),
        P("ctx", "head", None),
        P("ctx", "head", None),
        P(),
        P(),
        P("ctx"),
        P("ctx", "head", None),
    )
    return jax.shard_map(
        on_device,
        mesh=mesh,
        in_specs=placed,
        out_specs=(
            P("ctx", "head", None),
            P("ctx", "head", None),
            P("ctx", "head", None),
            P(),
            P(),
        ),
        check_vma=False,
    )
```

profile of v0, /device:TPU:1, one launch (start us, length us, event | category | flops | bytes accessed | tf_op | source)
XLA Modules:
  0.0 1427.9 jit_solution(4740694317553034300)
XLA Ops:
  7.2 1.3 fusion.43
  8.5 1.1 copy.39
  9.6 2.0 fusion.39
  12.4 1.7 fusion.28
  15.5 1.0 copy.38
  16.5 1.0 copy.47
  17.5 1.4 dynamic-slice
  20.5 261.6 %all-reduce.3 = (f32[128]{0:T(128)S(1)}, f32[128]{0:T(128)S(1)}) all-reduce(f32[128]{0:T(128)S(1)} %dynamic-update-slice, f32[128]{0:T(128)S(1)} %dynamic-update-slice.1), channel_id=1, replica_groups=mesh['ctx'=128,'head'=8] {'ctx'}, use_global_device_ids=true, to_apply=%add | all-reduce | flops 256 | bytes 2048
  283.0 1.2 broadcast_multiply_fusion
  284.5 451.2 %while.32 = (s32[]{:T(128)}, f32[2,128,128]{2,1,0:T(8,128)S(1)}, f32[]{:T(128)}, s32[]{:T(128)}, f32[128,2,128,128]{3,2,1,0:T(8,128)}, /*index=5*/f32[128]{0:T(128)S(1)}, s32[]{:T(128)}, f32[]{:T(128)}, s32[]{:T(128)}) while((s32[]{:T(128)}, f32[2,128,128]{2,1,0:T(8,128)S(1)}, f32[]{:T(128)}, s32[]{:T(128)}, ...), condition=%wide.region_1.2_spmd.clone, body=%wide.region_0.1_spmd.clone.sunk | while | flops 131082 | bytes 393401 | solution.py:23
  293.5 1.0 fusion.61
  318.4 1.0 fusion.61
  336.2 1.0 fusion.61
  343.3 1.0 fusion.61
  361.0 1.0 fusion.61
  385.9 1.0 fusion.61
  403.7 1.0 fusion.61
  410.8 1.0 fusion.61
  735.9 1.2 multiply_reduce_fusion
  739.7 1.1 fusion.4
  743.2 100.8 %all-gather.7.cloned.1.call-done = f32[256,128,128]{2,1,0:T(8,128)} async-done(((f32[2,128,128]{2,1,0:T(8,128)}), f32[256,128,128]{2,1,0:T(8,128)}) %all-gather.7.cloned.1.call-update) | async-done | bytes 16777232 | tf_op jit(solution)/shard_map/all_gather | solution.py:11
  844.0 11.6 rev.6
  855.7 451.2 %while.33 = (s32[]{:T(128)}, f32[2,128,128]{2,1,0:T(8,128)S(1)}, f32[]{:T(128)}, s32[]{:T(128)}, f32[128,2,128,128]{3,2,1,0:T(8,128)}, /*index=5*/f32[128]{0:T(128)S(1)}, s32[]{:T(128)}, f32[]{:T(128)}, s32[]{:T(128)}) while((s32[]{:T(128)}, f32[2,128,128]{2,1,0:T(8,128)S(1)}, f32[]{:T(128)}, s32[]{:T(128)}, ...), condition=%wide.region_5.6_spmd.clone, body=%wide.region_4.5_spmd.clone.sunk | while | flops 131082 | bytes 393401 | solution.py:23
  1308.3 112.3 %all-reduce.2 = (f32[128]{0:T(128)S(1)}, f32[128]{0:T(128)S(1)}) all-reduce(f32[128]{0:T(128)S(1)} %fusion.17, f32[128]{0:T(128)S(1)} %get-tuple-element.281), channel_id=1, replica_groups=mesh['ctx'=128,'head'=8] {'ctx','head'}, use_global_device_ids=true, to_apply=%region_7.8 | all-reduce | flops 256 | bytes 2048 | tf_op jit(solution)/shard_map/psum | solution.py:105
  (533 shorter events, 401.5 us)
Async XLA Ops:
  7.2 277.3 %all-gather.5.cloned.1.call-start = ((), (), s32[]{:S(2)}) async-start(), calls=%async_computation | async-start | bytes 16908288 | tf_op jit(solution)/shard_map/all_gather | solution.py:11
  14.1 829.9 %all-gather.7.cloned.1.call-start = ((), (), s32[]{:S(2)}) async-start(), calls=%async_computation.1 | async-start | bytes 16908288 | tf_op jit(solution)/shard_map/all_gather | solution.py:11
  844.0 462.9 %copy-start = (bf16[256,2,128]{2,1,0:T(2,128)(2,1)S(1)}, bf16[256,2,128]{2,1,0:T(2,128)(2,1)}, u32[]{:S(2)}) copy-start(bf16[256,2,128]{2,1,0:T(2,128)(2,1)} %param.13) | copy-start | bytes 393220
Sparse Core Ops, SparseCore 0:
  14.2 120.9 all-gather.4
  739.7 104.2 all-gather.6
where the time goes:
time: 1440 us; the launch traced here: 1430 us
  loops' own time  504 us (35%)
  blocking collectives  374 us (26%)
  other arithmetic  257 us (18%)
  local copies, waits for them, and re-layouts  170 us (12%)
  waiting for transfers between devices  101 us (7%)
  between operations  15.5 us (1%)
    another operation x2, loops' own time, entering(): return lax.fori_loop(0, count - 1, step, so_far)  504 us
    unnamed x1, blocking collectives  262 us
    select_n x254, other arithmetic, step(): jnp.where(position < mine, new, old)  250 us
    dynamic_slice x254, local copies, waits for them, and re-layouts, step(): longer = join(so_far, jax.tree.map(lambda part: part[position], pieces))  149 us
    psum x1, blocking collectives, on_device(): totals = lax.psum((thresh_term, gain_term), ('ctx', 'head'))  112 us
    all_gather x2, waiting for transfers between devices, entering(): pieces = jax.tree.map(lambda part: lax.all_gather(part, axis), value)  101 us
  transfers between devices with their start and end apart: 2, of which 1 were waited for; matrix products, arithmetic and copies ran while one was open for 1% of the time, Pallas kernels for 0%

commit v1 on v0

v1 whole, which is shorter than its diff:
```python
import functools
import math

import jax
import jax.numpy as jnp
from jax import lax
from jax.experimental import pallas as pl
from jax.experimental.pallas import tpu as pltpu
from jax.sharding import PartitionSpec as P

MESH = pl.DeviceIdType.MESH
F32 = jnp.float32
BF16 = jnp.bfloat16

ROW = 16


def mm(a, b, ca, cb):
    return lax.dot_general(a, b, (((ca,), (cb,)), ((), ())), preferred_element_type=F32)


def kernel(
    dims,
    docs_ref,
    thr_ref,
    gain_ref,
    q_hbm,
    spk_hbm,
    v_hbm,
    cot_hbm,
    att_hbm,
    qg_hbm,
    vg_hbm,
    grads_ref,
    q_in,
    spk_in,
    v_in,
    cot_in,
    q_st,
    v_st,
    cot_st,
    docT,
    mask,
    qb,
    kb,
    vb,
    gb,
    scores,
    base,
    vgrad,
    meta_my,
    meta,
    tail_f,
    recv_f,
    send_f,
    zs_f,
    zr_f,
    carr,
    tail_b,
    recv_b,
    send_b,
    zs_b,
    zr_b,
    retn,
    att_st,
    out_st,
    ar_x,
    ar_z,
    ar_y,
    att_out,
    qg_out,
    vg_out,
    in_sem,
    out_sem,
    meta_s,
    meta_r,
    st1_s,
    st1_r,
    st2_s,
    st2_r,
    st3_s,
    st3_r,
    st3_p,
    ar_s,
    ar_r,
):
    n_ctx, n_head, row_n, length, heads, width = dims
    chips = row_n // 2
    n_rows = n_ctx // row_n
    pr = width // chips
    me = lax.axis_index("ctx")
    my_y = lax.axis_index("head")
    my_row = me // row_n
    row0 = my_row * row_n
    pos = me - row0
    my_chip = pos // 2
    my_core = pos - my_chip * 2
    mid = chips // 2

    def peer_chip(t):
        turn = (t + 1) // 2
        d = mid + turn * (1 - 2 * (t - 2 * (t // 2)))
        return lax.rem(my_chip + d, chips)

    def in_row(p):
        return {"ctx": row0 + p}

    def along_z(k):
        return {"ctx": lax.rem(my_row + k, n_rows) * row_n + pos}

    def along_y(k):
        return {"head": lax.rem(my_y + k, n_head)}

    barrier = pltpu.get_barrier_semaphore()

    def greet_row(k, c):
        pl.semaphore_signal(
            barrier, inc=1, device_id=in_row(lax.rem(pos + k, row_n)), device_id_type=MESH
        )
        return c

    def greet_z(k, c):
        pl.semaphore_signal(barrier, inc=1, device_id=along_z(k), device_id_type=MESH)
        return c

    def greet_y(k, c):
        pl.semaphore_signal(barrier, inc=1, device_id=along_y(k), device_id_type=MESH)
        return c

    lax.fori_loop(1, row_n, greet_row, 0)
    lax.fori_loop(1, n_rows, greet_z, 0)
    if n_head > 1:
        lax.fori_loop(1, n_head, greet_y, 0)

    ins = [
        pltpu.make_async_copy(src, dst, in_sem.at[i])
        for i, (src, dst) in enumerate(
            ((spk_hbm, spk_in), (v_hbm, v_in), (q_hbm, q_in), (cot_hbm, cot_in))
        )
    ]
    for cp in ins:
        cp.start()

    doc_row = docs_ref[...].astype(F32)
    docT[...] = jnp.transpose(jnp.broadcast_to(doc_row, (width, length)))
    head_doc = docT[0:1, :]
    tail_doc = docT[length - 1 : length, :]
    sub = lax.broadcasted_iota(jnp.int32, (8, width), 0)
    meta_my[...] = jnp.where(
        sub == 0, jnp.broadcast_to(head_doc, (8, width)), jnp.broadcast_to(tail_doc, (8, width))
    )
    meta[pl.ds(pos, 1)] = meta_my[...].reshape(1, 8, width)
    thr = thr_ref[...]
    gain = gain_ref[...]
    thr_col = jnp.transpose(jnp.broadcast_to(thr, (width, width)))

    n_greet = (row_n - 1) + (n_rows - 1) + (n_head - 1)
    pl.semaphore_wait(barrier, n_greet)

    def send_meta(t, c):
        chip = peer_chip(t)
        for core in range(2):
            pltpu.make_async_remote_copy(
                src_ref=meta_my,
                dst_ref=meta.at[pos],
                send_sem=meta_s,
                recv_sem=meta_r,
                device_id=in_row(chip * 2 + core),
                device_id_type=MESH,
            ).start()
        return c

    lax.fori_loop(0, chips - 1, send_meta, 0)
    pltpu.make_async_remote_copy(
        src_ref=meta_my,
        dst_ref=meta.at[pos],
        send_sem=meta_s,
        recv_sem=meta_r,
        device_id=in_row(my_chip * 2 + 1 - my_core),
        device_id_type=MESH,
    ).start()

    def scatter(h, tail, recv, way):
        def piece(chip):
            return tail.at[pl.ds(h * width + chip * pr, pr)]

        def one(chip):
            pltpu.make_async_remote_copy(
                src_ref=piece(chip),
                dst_ref=recv.at[pos],
                send_sem=st1_s.at[way],
                recv_sem=st1_r.at[way],
                device_id=in_row(chip * 2 + h),
                device_id_type=MESH,
            ).start()

        def body(t, c):
            one(peer_chip(t))
            return c

        lax.fori_loop(0, chips - 1, body, 0)

        @pl.when(my_core != h)
        def _():
            one(my_chip)

        @pl.when(my_core == h)
        def _():
            recv[pl.ds(pos, 1)] = tail[pl.ds(h * width + my_chip * pr, pr), :].reshape(
                1, pr, width
            )

    def scatter_descriptor(recv, way):
        return pltpu.make_async_remote_copy(
            src_ref=recv.at[pl.ds(0, row_n - 1)],
            dst_ref=recv.at[pl.ds(0, row_n - 1)],
            send_sem=st1_s.at[way],
            recv_sem=st1_r.at[way],
            device_id=in_row(lax.rem(pos + 1, row_n)),
            device_id_type=MESH,
        )

    def gather(send, land, way):
        at = my_core * width + my_chip * pr

        def one(p, rsem):
            pltpu.make_async_remote_copy(
                src_ref=send.at[p],
                dst_ref=land.at[pl.ds(at, pr)],
                send_sem=st3_s.at[way],
                recv_sem=rsem,
                device_id=in_row(p),
                device_id_type=MESH,
            ).start()

        def body(t, c):
            chip = peer_chip(t)
            for core in range(2):
                one(chip * 2 + core, st3_r.at[way, my_core])
            return c

        lax.fori_loop(0, chips - 1, body, 0)
        one(my_chip * 2 + 1 - my_core, st3_p.at[way])
        land[pl.ds(at, pr), :] = send[pl.ds(pos, 1)].reshape(pr, width)

    def gather_wait_chips(land, way, h):
        part = land.at[pl.ds(0, (chips - 1) * pr)]
        pltpu.make_async_remote_copy(
            src_ref=part,
            dst_ref=part,
            send_sem=st3_s.at[way],
            recv_sem=st3_r.at[way, h],
            device_id=in_row(lax.rem(pos + 1, row_n)),
            device_id_type=MESH,
        ).wait_recv()

    def gather_wait_partner(land, way):
        part = land.at[pl.ds(0, pr)]
        pltpu.make_async_remote_copy(
            src_ref=part,
            dst_ref=part,
            send_sem=st3_s.at[way],
            recv_sem=st3_p.at[way],
            device_id=in_row(lax.rem(pos + 1, row_n)),
            device_id_type=MESH,
        ).wait_recv()

    def between_rows(k, zs, zr, slot, way):
        return pltpu.make_async_remote_copy(
            src_ref=zs,
            dst_ref=zr.at[slot],
            send_sem=st2_s.at[way, slot],
            recv_sem=st2_r.at[way, slot],
            device_id=along_z(k),
            device_id_type=MESH,
        )

    def with_mark(total, mark):
        return jnp.concatenate([total, jnp.broadcast_to(mark, (8, width))], axis=0)

    ins[0].wait()
    ins[1].wait()
    v_st[...] = v_in[...].astype(F32)
    first_f = (docT[...] == head_doc).astype(F32)
    last_f = (docT[...] == tail_doc).astype(F32)
    for h in range(heads):
        lane = pl.ds(h, length, stride=heads)
        spk = spk_in[lane, :].astype(F32)
        vals = v_st[lane, :].astype(BF16)
        vb[h] = vals
        tail_f[pl.ds(h * width, width), :] = mm((spk * last_f).astype(BF16), vals, 0, 0)
        kb[h] = (spk * thr).astype(BF16)
        scatter(h, tail_f, recv_f, 0)

    ins[2].wait()
    ins[3].wait()
    q_st[...] = q_in[...].astype(F32)
    cot_st[...] = cot_in[...].astype(F32)
    s_at = lax.broadcasted_iota(jnp.int32, (length, length), 0)
    t_at = lax.broadcasted_iota(jnp.int32, (length, length), 1)
    doc_s = jnp.concatenate([docT[...]] * (length // width), axis=1)
    mask[...] = ((t_at <= s_at) & (doc_s == doc_row)).astype(F32)
    for h in range(heads):
        lane = pl.ds(h, length, stride=heads)
        qf = q_st[lane, :]
        qb[h] = qf.astype(BF16)
        sc = (mm(qb[h], kb[h], 1, 1) * mask[...]).astype(BF16)
        scores[h] = sc
        base[h] = qf + mm(sc, vb[h], 1, 0)

    pltpu.make_async_remote_copy(
        src_ref=meta.at[pl.ds(0, row_n - 1)],
        dst_ref=meta.at[pl.ds(0, row_n - 1)],
        send_sem=meta_s,
        recv_sem=meta_r,
        device_id=in_row(lax.rem(pos + 1, row_n)),
        device_id_type=MESH,
    ).wait_recv()
    scatter_descriptor(recv_f, 0).wait_recv()
    run = recv_f[0]
    before = meta[0, 1:2, :]
    send_f[0] = jnp.zeros((pr, width), F32)
    for j in range(1, row_n):
        head_j, tail_j = meta[j, 0:1, :], meta[j, 1:2, :]
        send_f[j] = jnp.where(before == head_j, run, 0.0)
        run = recv_f[j] + jnp.where(before == tail_j, run, 0.0)
        before = tail_j
    zs_f[...] = with_mark(run, before)
    hops_f = [between_rows(k, zs_f, zr_f, k - 1, 0) for k in (1, 2)]
    for cp in hops_f:
        cp.start()
    for cp in hops_f:
        cp.wait_recv()
    z1, z2 = zr_f[0, 0:pr, :], zr_f[1, 0:pr, :]
    m1, m2 = zr_f[0, pr : pr + 1, :], zr_f[1, pr : pr + 1, :]
    for j in range(row_n):
        head_j = meta[j, 0:1, :]
        send_f[j] = (
            send_f[j] + jnp.where(m1 == head_j, z1, 0.0) + jnp.where(m2 == head_j, z2, 0.0)
        )
    gather(send_f, carr, 0)

    gain_term = jnp.zeros((1, width), F32)
    cross = jnp.zeros((1, width), F32)
    for h in range(heads):
        gather_wait_chips(carr, 0, h)
        if h == 0:
            gather_wait_partner(carr, 0)
        lane = pl.ds(h, length, stride=heads)
        state = (carr[pl.ds(h * width, width), :] * thr_col).astype(BF16)
        mixed = base[h] + first_f * mm(qb[h], state, 1, 0)
        ratio = lax.rsqrt(jnp.mean(mixed * mixed, axis=-1, keepdims=True) + 1e-06)
        normed = mixed * ratio
        cot = cot_st[lane, :]
        upstream = cot * gain
        g = (
            ratio * upstream - normed * (ratio * jnp.mean(normed * upstream, axis=-1, keepdims=True))
        ).astype(BF16)
        gb[h] = g
        tail_b[pl.ds(h * width, width), :] = mm((q_st[lane, :] * first_f).astype(BF16), g, 0, 0)
        scatter(h, tail_b, recv_b, 1)
        att_st[lane, :] = normed * gain
        gain_term = gain_term + jnp.sum(cot * normed, axis=0, keepdims=True)

    att_out[...] = att_st[...].astype(BF16)
    outs = [pltpu.make_async_copy(att_out, att_hbm, out_sem.at[0])]
    outs[0].start()
    for h in range(heads):
        lane = pl.ds(h, length, stride=heads)
        rows = pl.ds(h * width, width)
        cs = carr[rows, :]
        cross = cross + jnp.sum(jnp.transpose(tail_b[rows, :] * cs), axis=0, keepdims=True)
        state = (cs * thr_col).astype(BF16)
        g = gb[h]
        ds = (mm(g, vb[h], 1, 1) * mask[...]).astype(BF16)
        out_st[lane, :] = g.astype(F32) + mm(ds, kb[h], 1, 0) + first_f * mm(g, state, 1, 1)
        kg = mm(ds, qb[h], 0, 0)
        cross = cross + jnp.sum(spk_in[lane, :].astype(F32) * kg, axis=0, keepdims=True)
        vgrad[h] = mm(scores[h], g, 0, 0)

    def total_copy(buf, mine, stage, device):
        return pltpu.make_async_remote_copy(
            src_ref=buf.at[mine],
            dst_ref=buf.at[mine],
            send_sem=ar_s.at[stage],
            recv_sem=ar_r.at[stage],
            device_id=device,
            device_id_type=MESH,
        )

    def total_start(buf, count, mine, stage, device, value):
        buf[pl.ds(mine, 1)] = value.reshape(1, 8, width)

        def body(k, c):
            total_copy(buf, mine, stage, device(k)).start()
            return c

        lax.fori_loop(1, count, body, 0)

    def total_descriptor(buf, count, stage, device):
        part = buf.at[pl.ds(0, count - 1)]
        return pltpu.make_async_remote_copy(
            src_ref=part,
            dst_ref=part,
            send_sem=ar_s.at[stage],
            recv_sem=ar_r.at[stage],
            device_id=device(1),
            device_id_type=MESH,
        )

    def row_peer(k):
        return in_row(lax.rem(pos + k, row_n))

    partial = jnp.where(
        sub == 0, jnp.broadcast_to(cross, (8, width)), jnp.broadcast_to(gain_term, (8, width))
    )
    total_start(ar_x, row_n, pos, 0, row_peer, partial)
    qg_out[...] = out_st[...].astype(BF16)
    outs.append(pltpu.make_async_copy(qg_out, qg_hbm, out_sem.at[1]))
    outs[1].start()

    scatter_descriptor(recv_b, 1).wait_recv()
    run = recv_b[row_n - 1]
    after = meta[row_n - 1, 0:1, :]
    send_b[row_n - 1] = jnp.zeros((pr, width), F32)
    for j in range(row_n - 2, -1, -1):
        head_j, tail_j = meta[j, 0:1, :], meta[j, 1:2, :]
        send_b[j] = jnp.where(after == tail_j, run, 0.0)
        run = recv_b[j] + jnp.where(after == head_j, run, 0.0)
        after = head_j
    zs_b[...] = with_mark(run, after)
    hops_b = [between_rows(n_rows - k, zs_b, zr_b, k - 1, 1) for k in (1, 2)]
    for cp in hops_b:
        cp.start()

    total_descriptor(ar_x, row_n, 0, row_peer).wait_recv()
    total_start(ar_z, n_rows, my_row, 1, along_z, jnp.sum(ar_x[...], axis=0))

    for cp in hops_b:
        cp.wait_recv()
    z1, z2 = zr_b[0, 0:pr, :], zr_b[1, 0:pr, :]
    m1, m2 = zr_b[0, pr : pr + 1, :], zr_b[1, pr : pr + 1, :]
    for j in range(row_n):
        tail_j = meta[j, 1:2, :]
        send_b[j] = (
            send_b[j] + jnp.where(m1 == tail_j, z1, 0.0) + jnp.where(m2 == tail_j, z2, 0.0)
        )
    gather(send_b, retn, 1)

    total_descriptor(ar_z, n_rows, 1, along_z).wait_recv()
    by_row = jnp.sum(ar_z[...], axis=0)
    if n_head > 1:
        total_start(ar_y, n_head, my_y, 2, along_y, by_row)

    for h in range(heads):
        gather_wait_chips(retn, 1, h)
        if h == 0:
            gather_wait_partner(retn, 1)
        lane = pl.ds(h, length, stride=heads)
        state = retn[pl.ds(h * width, width), :].astype(BF16)
        out_st[lane, :] = vgrad[h] + last_f * mm(kb[h], state, 1, 0)
    vg_out[...] = out_st[...].astype(BF16)
    outs.append(pltpu.make_async_copy(vg_out, vg_hbm, out_sem.at[2]))
    outs[2].start()

    if n_head > 1:
        total_descriptor(ar_y, n_head, 2, along_y).wait_recv()
        by_row = jnp.sum(ar_y[...], axis=0)
    scale = 1.0 / math.sqrt(length * n_ctx * heads * n_head)
    grads_ref[...] = by_row * scale

    for cp in outs:
        cp.wait()
    pltpu.make_async_remote_copy(
        src_ref=meta.at[pl.ds(0, row_n - 1)],
        dst_ref=meta.at[pl.ds(0, row_n - 1)],
        send_sem=meta_s,
        recv_sem=meta_r,
        device_id=row_peer(1),
        device_id_type=MESH,
    ).wait_send()
    for way, recv, send in ((0, recv_f, send_f), (1, recv_b, send_b)):
        scatter_descriptor(recv, way).wait_send()
        pltpu.make_async_remote_copy(
            src_ref=send.at[pl.ds(0, row_n - 1)],
            dst_ref=send.at[pl.ds(0, row_n - 1)],
            send_sem=st3_s.at[way],
            recv_sem=st3_r.at[way, 0],
            device_id=row_peer(1),
            device_id_type=MESH,
        ).wait_send()
    for cp in hops_f + hops_b:
        cp.wait_send()
    total_descriptor(ar_x, row_n, 0, row_peer).wait_send()
    total_descriptor(ar_z, n_rows, 1, along_z).wait_send()
    if n_head > 1:
        total_descriptor(ar_y, n_head, 2, along_y).wait_send()


def on_device(n_ctx, n_head, queries, spikes, values, threshold, norm_gain, document_ids, cotangent):
    length, heads, width = queries.shape
    dims = (n_ctx, n_head, ROW, length, heads, width)
    n_rows = n_ctx // ROW
    pr = width // (ROW // 2)
    flat = (length * heads, width)
    state = (heads * width, width)
    vmem = pl.BlockSpec(memory_space=pltpu.VMEM)
    hbm = pl.BlockSpec(memory_space=pl.ANY)
    dma = pltpu.SemaphoreType.DMA
    one_way = [
        pltpu.VMEM(state, F32),
        pltpu.VMEM((ROW, pr, width), F32),
        pltpu.VMEM((ROW, pr, width), F32),
        pltpu.VMEM((pr + 8, width), F32),
        pltpu.VMEM((2, pr + 8, width), F32),
        pltpu.VMEM(state, F32),
    ]
    att, qg, vg, grads = pl.pallas_call(
        functools.partial(kernel, dims),
        out_shape=[jax.ShapeDtypeStruct(flat, BF16)] * 3 + [jax.ShapeDtypeStruct((8, width), F32)],
        in_specs=[vmem] * 3 + [hbm] * 4,
        out_specs=[hbm] * 3 + [vmem],
        scratch_shapes=[
            pltpu.VMEM(flat, BF16),
            pltpu.VMEM(flat, jnp.int32),
            pltpu.VMEM(flat, BF16),
            pltpu.VMEM(flat, BF16),
            pltpu.VMEM(flat, F32),
            pltpu.VMEM(flat, F32),
            pltpu.VMEM(flat, F32),
            pltpu.VMEM((length, width), F32),
            pltpu.VMEM((length, length), F32),
            pltpu.VMEM((heads, length, width), BF16),
            pltpu.VMEM((heads, length, width), BF16),
            pltpu.VMEM((heads, length, width), BF16),
            pltpu.VMEM((heads, length, width), BF16),
            pltpu.VMEM((heads, length, length), BF16),
            pltpu.VMEM((heads, length, width), F32),
            pltpu.VMEM((heads, length, width), F32),
            pltpu.VMEM((8, width), F32),
            pltpu.VMEM((ROW, 8, width), F32),
            *one_way,
            *one_way,
            pltpu.VMEM(flat, F32),
            pltpu.VMEM(flat, F32),
            pltpu.VMEM((ROW, 8, width), F32),
            pltpu.VMEM((n_rows, 8, width), F32),
            pltpu.VMEM((max(n_head, 2), 8, width), F32),
            pltpu.VMEM(flat, BF16),
            pltpu.VMEM(flat, BF16),
            pltpu.VMEM(flat, BF16),
            dma((4,)),
            dma((3,)),
            dma,
            dma,
            dma((2,)),
            dma((2,)),
            dma((2, 2)),
            dma((2, 2)),
            dma((2,)),
            dma((2, 2)),
            dma((2,)),
            dma((3,)),
            dma((3,)),
        ],
        compiler_params=pltpu.CompilerParams(collective_id=0, has_side_effects=True),
    )(
        document_ids.reshape(1, length),
        threshold.reshape(1, width),
        norm_gain.reshape(1, width),
        queries.reshape(flat),
        spikes.reshape(flat),
        values.reshape(flat),
        cotangent.reshape(flat),
    )
    whole = (length, heads, width)
    return att.reshape(whole), qg.reshape(whole), vg.reshape(whole), grads[0], grads[1]


def solution(mesh):
    tokens = P("ctx", "head", None)
    return jax.shard_map(
        functools.partial(on_device, mesh.shape["ctx"], mesh.shape["head"]),
        mesh=mesh,
        in_specs=(tokens, tokens, tokens, P(), P(), P("ctx"), tokens),
        out_specs=(tokens, tokens, tokens, P(), P()),
        check_vma=False,
    )
```

time: 1440 us -> 62.9 us (0.04)
  loops' own time: 504 us -> 0 us
  blocking collectives: 374 us -> 0 us
  other arithmetic: 257 us -> 0 us
  local copies, waits for them, and re-layouts: 170 us -> 4.56 us
  waiting for transfers between devices: 101 us -> 0 us
  Pallas kernels: 0 us -> 57.2 us
  between operations: 15.5 us -> 0.65 us
    another operation x2 -> x0, loops' own time: 504 us -> none  [entering(): return lax.fori_loop(0, count - 1, step, so_far)]
    unnamed x1 -> x0, blocking collectives: 262 us -> none
    select_n x254 -> x0, other arithmetic: 250 us -> none  [step(): jnp.where(position < mine, new, old)]
    dynamic_slice x254 -> x0, local copies, waits for them, and re-layouts: 149 us -> none  [step(): longer = join(so_far, jax.tree.map(lambda part: part[position], pieces))]
    psum x1 -> x0, blocking collectives: 112 us -> none  [on_device(): totals = lax.psum((thresh_term, gain_term), ('ctx', 'head'))]
    all_gather x2 -> x0, waiting for transfers between devices: 101 us -> none  [entering(): pieces = jax.tree.map(lambda part: lax.all_gather(part, axis), value)]
    pallas_call x0 -> x1, Pallas kernels: none -> 57.2 us  [on_device(): pl.pallas_call(functools.partial(kernel, dims), out_shape=[jax.ShapeDtype...]
  transfers between devices with their start and end apart: 2 -> 0, of which waited for: 1 -> 0; matrix products, arithmetic and copies ran while one was open for 1% -> 0% of each run, Pallas kernels for 0% -> 0%
where the time goes in v1:
time: 62.9 us; the launch traced here: 62.4 us
  Pallas kernels  57.2 us (91%)
  local copies, waits for them, and re-layouts  4.56 us (7%)
  between operations  0.65 us (1%)
    pallas_call x1, Pallas kernels, on_device(): pl.pallas_call(functools.partial(kernel, dims), out_shape=[jax.ShapeDtype...  57.2 us
    unnamed x7, local copies, waits for them, and re-layouts  3.29 us
    squeeze x1, local copies, waits for them, and re-layouts, on_device(): grads[1]  1.27 us

profile of v1, /device:TPU:1, one launch (start us, length us, event | category | flops | bytes accessed | tf_op | source)
XLA Modules:
  0.0 62.4 jit_solution(10337981453779505363)
XLA Ops:
  0.6 57.2 %shard_map.110 = (bf16[512,128]{1,0:T(8,128)(2,1)}, bf16[512,128]{1,0:T(8,128)(2,1)}, bf16[512,128]{1,0:T(8,128)(2,1)}, f32[8,128]{1,0:T(8,128)}) custom-call(s32[1,256]{1,0:T(1,128)} %bitcast.21, f32[1,128]{1,0:T(1,128)} %bitcast.22, f32[1,128]{1,0:T(1,128)} %bitcast.23, bf16[512,128]{1,0:T(8,128)(2,1)} %bitcast.15, s32[512,128]{1,0:T(8,128)} %bitcast.14, ...), custom_call_target="tpu_custom_call" | custom-call | tf_op jit(solution)/shard_map/pallas_call | solution.py:518
  57.9 1.3 %slice_bitcast_fusion = (f32[128]{0:T(128)}, f32[128]{0:T(128)}) fusion(f32[8,128]{1,0:T(8,128)} %get-tuple-element.12), kind=kLoop, calls=%fused_computation | loop fusion | bytes 2048 | tf_op jit(solution)/shard_map/squeeze | solution.py:577
  59.1 0.0 copy-start.1
  59.1 1.7 %copy.15 = bf16[256,2,128]{2,1,0:T(2,128)(2,1)} copy(bf16[256,2,128]{2,1,0:T(2,128)(2,1)} %bitcast.20) | data formatting | bytes 262144
  60.8 0.0 copy-done.1
  60.8 0.0 copy-start
  60.8 0.7 %copy.16 = bf16[256,2,128]{2,1,0:T(2,128)(2,1)} copy(bf16[256,2,128]{2,1,0:T(2,128)(2,1)S(1)} %bitcast.19) | data formatting | bytes 262144
  61.5 0.3 copy-done
  61.8 0.7 %copy.17 = bf16[256,2,128]{2,1,0:T(2,128)(2,1)} copy(bf16[256,2,128]{2,1,0:T(2,128)(2,1)S(1)} %bitcast.18) | data formatting | bytes 262144
Async XLA Ops:
  59.1 1.7 %copy-start.1 = (bf16[512,128]{1,0:T(8,128)(2,1)S(1)}, bf16[512,128]{1,0:T(8,128)(2,1)}, u32[]{:S(2)}) copy-start(bf16[512,128]{1,0:T(8,128)(2,1)} %get-tuple-element.10) | copy-start | bytes 393220
  60.8 1.0 %copy-start = (bf16[512,128]{1,0:T(8,128)(2,1)S(1)}, bf16[512,128]{1,0:T(8,128)(2,1)}, u32[]{:S(2)}) copy-start(bf16[512,128]{1,0:T(8,128)(2,1)} %get-tuple-element.11) | copy-start | bytes 393220

commit v2 on v1

--- a/solution.py
+++ b/solution.py
@@ -21,17 +21,20 @@
 
 def kernel(
     dims,
-    docs_ref,
-    thr_ref,
-    gain_ref,
+    docs_hbm,
+    thr_hbm,
+    gain_hbm,
     q_hbm,
     spk_hbm,
     v_hbm,
     cot_hbm,
-    att_hbm,
-    qg_hbm,
-    vg_hbm,
+    att_ref,
+    qg_ref,
+    vg_ref,
     grads_ref,
+    docs_in,
+    thr_in,
+    gain_in,
     q_in,
     spk_in,
     v_in,
@@ -46,6 +49,7 @@
     vb,
     gb,
     scores,
+    dscores,
     base,
     vgrad,
     meta_my,
@@ -67,11 +71,7 @@
     ar_x,
     ar_z,
     ar_y,
-    att_out,
-    qg_out,
-    vg_out,
     in_sem,
-    out_sem,
     meta_s,
     meta_r,
     st1_s,
@@ -83,6 +83,8 @@
     st3_p,
     ar_s,
     ar_r,
+    token,
+    hello,
 ):
     n_ctx, n_head, row_n, length, heads, width = dims
     chips = row_n // 2
@@ -105,11 +107,31 @@
     def in_row(p):
         return {"ctx": row0 + p}
 
+    def to_row(r):
+        return {"ctx": r * row_n + pos}
+
     def along_z(k):
         return {"ctx": lax.rem(my_row + k, n_rows) * row_n + pos}
 
     def along_y(k):
         return {"head": lax.rem(my_y + k, n_head)}
+
+    ins = [
+        pltpu.make_async_copy(src, dst, in_sem.at[i])
+        for i, (src, dst) in enumerate(
+            (
+                (docs_hbm, docs_in),
+                (thr_hbm, thr_in),
+                (spk_hbm, spk_in),
+                (v_hbm, v_in),
+                (q_hbm, q_in),
+                (cot_hbm, cot_in),
+                (gain_hbm, gain_in),
+            )
+        )
+    ]
+    for cp in ins:
+        cp.start()
 
     barrier = pltpu.get_barrier_semaphore()
 
@@ -119,43 +141,48 @@
         )
         return c
 
-    def greet_z(k, c):
-        pl.semaphore_signal(barrier, inc=1, device_id=along_z(k), device_id_type=MESH)
-        return c
-
     def greet_y(k, c):
         pl.semaphore_signal(barrier, inc=1, device_id=along_y(k), device_id_type=MESH)
         return c
 
     lax.fori_loop(1, row_n, greet_row, 0)
-    lax.fori_loop(1, n_rows, greet_z, 0)
+    for k in (1, 2):
+
+        @pl.when(my_row >= k)
+        def _():
+            pl.semaphore_signal(barrier, inc=1, device_id=to_row(my_row - k), device_id_type=MESH)
+
+        @pl.when(my_row + k < n_rows)
+        def _():
+            pl.semaphore_signal(barrier, inc=1, device_id=to_row(my_row + k), device_id_type=MESH)
+
     if n_head > 1:
         lax.fori_loop(1, n_head, greet_y, 0)
 
-    ins = [
-        pltpu.make_async_copy(src, dst, in_sem.at[i])
-        for i, (src, dst) in enumerate(
-            ((spk_hbm, spk_in), (v_hbm, v_in), (q_hbm, q_in), (cot_hbm, cot_in))
-        )
-    ]
-    for cp in ins:
-        cp.start()
-
-    doc_row = docs_ref[...].astype(F32)
+    for k in range(2):
+
+        @pl.when(my_row <= k)
+        def _():
+            zr_f[k] = jnp.full((pr + 8, width), -1.0, F32)
+
+        @pl.when(my_row + k >= n_rows - 1)
+        def _():
+            zr_b[k] = jnp.full((pr + 8, width), -1.0, F32)
+
+    ins[0].wait()
+    ins[1].wait()
+    doc_row = docs_in[...].astype(F32)
     docT[...] = jnp.transpose(jnp.broadcast_to(doc_row, (width, length)))
     head_doc = docT[0:1, :]
     tail_doc = docT[length - 1 : length, :]
-    sub = lax.broadcasted_iota(jnp.int32, (8, width), 0)
-    meta_my[...] = jnp.where(
-        sub == 0, jnp.broadcast_to(head_doc, (8, width)), jnp.broadcast_to(tail_doc, (8, width))
-    )
-    meta[pl.ds(pos, 1)] = meta_my[...].reshape(1, 8, width)
-    thr = thr_ref[...]
-    gain = gain_ref[...]
+    ends = jnp.concatenate([head_doc, tail_doc], axis=0)
+    meta_my[...] = ends
+    meta[pl.ds(pos, 1)] = ends.reshape(1, 2, width)
+    thr = thr_in[...]
     thr_col = jnp.transpose(jnp.broadcast_to(thr, (width, width)))
 
-    n_greet = (row_n - 1) + (n_rows - 1) + (n_head - 1)
-    pl.semaphore_wait(barrier, n_greet)
+    near = jnp.minimum(my_row, 2) + jnp.minimum(n_rows - 1 - my_row, 2)
+    pl.semaphore_wait(barrier, (row_n - 1) + (n_head - 1) + near)
 
     def send_meta(t, c):
         chip = peer_chip(t)
@@ -265,21 +292,37 @@
             device_id_type=MESH,
         ).wait_recv()
 
-    def between_rows(k, zs, zr, slot, way):
-        return pltpu.make_async_remote_copy(
+    def row_hop(k, zs, zr, way):
+        step = k * (1 - 2 * way)
+        copy = pltpu.make_async_remote_copy(
             src_ref=zs,
-            dst_ref=zr.at[slot],
-            send_sem=st2_s.at[way, slot],
-            recv_sem=st2_r.at[way, slot],
-            device_id=along_z(k),
+            dst_ref=zr.at[k - 1],
+            send_sem=st2_s.at[way, k - 1],
+            recv_sem=st2_r.at[way, k - 1],
+            device_id=to_row(my_row + step),
             device_id_type=MESH,
         )
+        ahead = my_row + k < n_rows
+        behind = my_row >= k
+        return (copy, behind, ahead) if way else (copy, ahead, behind)
+
+    def hops_start(hops):
+        for copy, sends, _ in hops:
+            pl.when(sends)(copy.start)
+
+    def hops_wait_recv(hops):
+        for copy, _, receives in hops:
+            pl.when(receives)(copy.wait_recv)
+
+    def hops_wait_send(hops):
+        for copy, sends, _ in hops:
+            pl.when(sends)(copy.wait_send)
 
     def with_mark(total, mark):
         return jnp.concatenate([total, jnp.broadcast_to(mark, (8, width))], axis=0)
 
-    ins[0].wait()
-    ins[1].wait()
+    ins[2].wait()
+    ins[3].wait()
     v_st[...] = v_in[...].astype(F32)
     first_f = (docT[...] == head_doc).astype(F32)
     last_f = (docT[...] == tail_doc).astype(F32)
@@ -292,8 +335,9 @@
         kb[h] = (spk * thr).astype(BF16)
         scatter(h, tail_f, recv_f, 0)
 
-    ins[2].wait()
-    ins[3].wait()
+    for cp in ins[4:]:
+        cp.wait()
+    gain = gain_in[...]
     q_st[...] = q_in[...].astype(F32)
     cot_st[...] = cot_in[...].astype(F32)
     s_at = lax.broadcasted_iota(jnp.int32, (length, length), 0)
@@ -326,11 +370,9 @@
         run = recv_f[j] + jnp.where(before == tail_j, run, 0.0)
         before = tail_j
     zs_f[...] = with_mark(run, before)
-    hops_f = [between_rows(k, zs_f, zr_f, k - 1, 0) for k in (1, 2)]
-    for cp in hops_f:
-        cp.start()
-    for cp in hops_f:
-        cp.wait_recv()
+    hops_f = [row_hop(k, zs_f, zr_f, 0) for k in (1, 2)]
+    hops_start(hops_f)
+    hops_wait_recv(hops_f)
     z1, z2 = zr_f[0, 0:pr, :], zr_f[1, 0:pr, :]
     m1, m2 = zr_f[0, pr : pr + 1, :], zr_f[1, pr : pr + 1, :]
     for j in range(row_n):
@@ -339,6 +381,20 @@
             send_f[j] + jnp.where(m1 == head_j, z1, 0.0) + jnp.where(m2 == head_j, z2, 0.0)
         )
     gather(send_f, carr, 0)
+
+    @pl.when(my_row > 0)
+    def _():
+        pl.semaphore_wait(token, 1)
+
+    @pl.when(my_row < n_rows - 1)
+    def _():
+        pl.semaphore_signal(token, inc=1, device_id=to_row(my_row + 1), device_id_type=MESH)
+
+    def greet_below(r, c):
+        pl.semaphore_signal(hello, inc=1, device_id=to_row(r), device_id_type=MESH)
+        return c
+
+    lax.fori_loop(0, my_row, greet_below, 0)
 
     gain_term = jnp.zeros((1, width), F32)
     cross = jnp.zeros((1, width), F32)
@@ -358,25 +414,8 @@
         ).astype(BF16)
         gb[h] = g
         tail_b[pl.ds(h * width, width), :] = mm((q_st[lane, :] * first_f).astype(BF16), g, 0, 0)
-        scatter(h, tail_b, recv_b, 1)
         att_st[lane, :] = normed * gain
         gain_term = gain_term + jnp.sum(cot * normed, axis=0, keepdims=True)
-
-    att_out[...] = att_st[...].astype(BF16)
-    outs = [pltpu.make_async_copy(att_out, att_hbm, out_sem.at[0])]
-    outs[0].start()
-    for h in range(heads):
-        lane = pl.ds(h, length, stride=heads)
-        rows = pl.ds(h * width, width)
-        cs = carr[rows, :]
-        cross = cross + jnp.sum(jnp.transpose(tail_b[rows, :] * cs), axis=0, keepdims=True)
-        state = (cs * thr_col).astype(BF16)
-        g = gb[h]
-        ds = (mm(g, vb[h], 1, 1) * mask[...]).astype(BF16)
-        out_st[lane, :] = g.astype(F32) + mm(ds, kb[h], 1, 0) + first_f * mm(g, state, 1, 1)
-        kg = mm(ds, qb[h], 0, 0)
-        cross = cross + jnp.sum(spk_in[lane, :].astype(F32) * kg, axis=0, keepdims=True)
-        vgrad[h] = mm(scores[h], g, 0, 0)
 
     def total_copy(buf, mine, stage, device):
         return pltpu.make_async_remote_copy(
@@ -389,7 +428,7 @@
         )
 
     def total_start(buf, count, mine, stage, device, value):
-        buf[pl.ds(mine, 1)] = value.reshape(1, 8, width)
+        buf[pl.ds(mine, 1)] = value.reshape(1, 2, width)
 
         def body(k, c):
             total_copy(buf, mine, stage, device(k)).start()
@@ -411,13 +450,36 @@
     def row_peer(k):
         return in_row(lax.rem(pos + k, row_n))
 
-    partial = jnp.where(
-        sub == 0, jnp.broadcast_to(cross, (8, width)), jnp.broadcast_to(gain_term, (8, width))
-    )
-    total_start(ar_x, row_n, pos, 0, row_peer, partial)
-    qg_out[...] = out_st[...].astype(BF16)
-    outs.append(pltpu.make_async_copy(qg_out, qg_hbm, out_sem.at[1]))
-    outs[1].start()
+    for h in range(heads):
+        lane = pl.ds(h, length, stride=heads)
+        rows = pl.ds(h * width, width)
+        cross = cross + jnp.sum(
+            jnp.transpose(tail_b[rows, :] * carr[rows, :]), axis=0, keepdims=True
+        )
+        ds = (mm(gb[h], vb[h], 1, 1) * mask[...]).astype(BF16)
+        dscores[h] = ds
+        kg = mm(ds, qb[h], 0, 0)
+        cross = cross + jnp.sum(spk_in[lane, :].astype(F32) * kg, axis=0, keepdims=True)
+    total_start(ar_x, row_n, pos, 0, row_peer, jnp.concatenate([cross, gain_term], axis=0))
+
+    for h in range(heads):
+        scatter(h, tail_b, recv_b, 1)
+
+    att_ref[...] = att_st[...].astype(BF16)
+    for h in range(heads):
+        lane = pl.ds(h, length, stride=heads)
+        state = (carr[pl.ds(h * width, width), :] * thr_col).astype(BF16)
+        g = gb[h]
+        out_st[lane, :] = (
+            g.astype(F32) + mm(dscores[h], kb[h], 1, 0) + first_f * mm(g, state, 1, 1)
+        )
+        vgrad[h] = mm(scores[h], g, 0, 0)
+    qg_ref[...] = out_st[...].astype(BF16)
+
+    total_descriptor(ar_x, row_n, 0, row_peer).wait_recv()
+    total = jnp.sum(ar_x[...], axis=0)
+    if n_head > 1:
+        total_start(ar_y, n_head, my_y, 1, along_y, total)
 
     scatter_descriptor(recv_b, 1).wait_recv()
     run = recv_b[row_n - 1]
@@ -429,15 +491,20 @@
         run = recv_b[j] + jnp.where(after == head_j, run, 0.0)
         after = head_j
     zs_b[...] = with_mark(run, after)
-    hops_b = [between_rows(n_rows - k, zs_b, zr_b, k - 1, 1) for k in (1, 2)]
-    for cp in hops_b:
-        cp.start()
-
-    total_descriptor(ar_x, row_n, 0, row_peer).wait_recv()
-    total_start(ar_z, n_rows, my_row, 1, along_z, jnp.sum(ar_x[...], axis=0))
-
-    for cp in hops_b:
-        cp.wait_recv()
+    hops_b = [row_hop(k, zs_b, zr_b, 1) for k in (1, 2)]
+    hops_start(hops_b)
+
+    if n_head > 1:
+        total_descriptor(ar_y, n_head, 1, along_y).wait_recv()
+        total = jnp.sum(ar_y[...], axis=0)
+
+    @pl.when(my_row < n_rows - 1)
+    def _():
+        pl.semaphore_wait(hello, n_rows - 1 - my_row)
+
+    total_start(ar_z, n_rows, my_row, 2, along_z, total)
+
+    hops_wait_recv(hops_b)
     z1, z2 = zr_b[0, 0:pr, :], zr_b[1, 0:pr, :]
     m1, m2 = zr_b[0, pr : pr + 1, :], zr_b[1, pr : pr + 1, :]
     for j in range(row_n):
@@ -446,11 +513,6 @@
             send_b[j] + jnp.where(m1 == tail_j, z1, 0.0) + jnp.where(m2 == tail_j, z2, 0.0)
         )
     gather(send_b, retn, 1)
-
-    total_descriptor(ar_z, n_rows, 1, along_z).wait_recv()
-    by_row = jnp.sum(ar_z[...], axis=0)
-    if n_head > 1:
-        total_start(ar_y, n_head, my_y, 2, along_y, by_row)
 
     for h in range(heads):
         gather_wait_chips(retn, 1, h)
@@ -459,18 +521,12 @@
         lane = pl.ds(h, length, stride=heads)
         state = retn[pl.ds(h * width, width), :].astype(BF16)
         out_st[lane, :] = vgrad[h] + last_f * mm(kb[h], state, 1, 0)
-    vg_out[...] = out_st[...].astype(BF16)
-    outs.append(pltpu.make_async_copy(vg_out, vg_hbm, out_sem.at[2]))
-    outs[2].start()
-
-    if n_head > 1:
-        total_descriptor(ar_y, n_head, 2, along_y).wait_recv()
-        by_row = jnp.sum(ar_y[...], axis=0)
+    vg_ref[...] = out_st[...].astype(BF16)
+
+    total_descriptor(ar_z, n_rows, 2, along_z).wait_recv()
     scale = 1.0 / math.sqrt(length * n_ctx * heads * n_head)
-    grads_ref[...] = by_row * scale
-
-    for cp in outs:
-        cp.wait()
+    grads_ref[...] = jnp.sum(ar_z[...], axis=0) * scale
+
     pltpu.make_async_remote_copy(
         src_ref=meta.at[pl.ds(0, row_n - 1)],
         dst_ref=meta.at[pl.ds(0, row_n - 1)],
@@ -489,12 +545,26 @@
             device_id=row_peer(1),
             device_id_type=MESH,
         ).wait_send()
-    for cp in hops_f + hops_b:
-        cp.wait_send()
+    hops_wait_send(hops_f + hops_b)
     total_descriptor(ar_x, row_n, 0, row_peer).wait_send()
-    total_descriptor(ar_z, n_rows, 1, along_z).wait_send()
+    total_descriptor(ar_z, n_rows, 2, along_z).wait_send()
     if n_head > 1:
-        total_descriptor(ar_y, n_head, 2, along_y).wait_send()
+        total_descriptor(ar_y, n_head, 1, along_y).wait_send()
+
+
+def put_out(att, qg, vg, grads, att_hbm, qg_hbm, vg_hbm, thr_hbm, gain_hbm, sem):
+    pairs = (
+        (att, att_hbm),
+        (qg, qg_hbm),
+        (vg, vg_hbm),
+        (grads.at[pl.ds(0, 1)], thr_hbm),
+        (grads.at[pl.ds(1, 1)], gain_hbm),
+    )
+    copies = [pltpu.make_async_copy(src, dst, sem.at[i]) for i, (src, dst) in enumerate(pairs)]
+    for copy in copies:
+        copy.start()
+    for copy in copies:
+        copy.wait()
 
 
 def on_device(n_ctx, n_head, queries, spikes, values, threshold, norm_gain, document_ids, cotangent):
@@ -515,12 +585,15 @@
         pltpu.VMEM((2, pr + 8, width), F32),
         pltpu.VMEM(state, F32),
     ]
-    att, qg, vg, grads = pl.pallas_call(
+    results = pl.pallas_call(
         functools.partial(kernel, dims),
-        out_shape=[jax.ShapeDtypeStruct(flat, BF16)] * 3 + [jax.ShapeDtypeStruct((8, width), F32)],
-        in_specs=[vmem] * 3 + [hbm] * 4,
-        out_specs=[hbm] * 3 + [vmem],
+        out_shape=[pltpu.VMEM(flat, BF16)] * 3 + [pltpu.VMEM((2, width), F32)],
+        in_specs=[hbm] * 7,
+        out_specs=[vmem] * 4,
         scratch_shapes=[
+            pltpu.VMEM((1, length), jnp.int32),
+            pltpu.VMEM((1, width), F32),
+            pltpu.VMEM((1, width), F32),
             pltpu.VMEM(flat, BF16),
             pltpu.VMEM(flat, jnp.int32),
             pltpu.VMEM(flat, BF16),
@@ -535,22 +608,19 @@
             pltpu.VMEM((heads, length, width), BF16),
             pltpu.VMEM((heads, length, width), BF16),
             pltpu.VMEM((heads, length, length), BF16),
+            pltpu.VMEM((heads, length, length), BF16),
             pltpu.VMEM((heads, length, width), F32),
             pltpu.VMEM((heads, length, width), F32),
-            pltpu.VMEM((8, width), F32),
-            pltpu.VMEM((ROW, 8, width), F32),
+            pltpu.VMEM((2, width), F32),
+            pltpu.VMEM((ROW, 2, width), F32),
             *one_way,
             *one_way,
             pltpu.VMEM(flat, F32),
             pltpu.VMEM(flat, F32),
-            pltpu.VMEM((ROW, 8, width), F32),
-            pltpu.VMEM((n_rows, 8, width), F32),
-            pltpu.VMEM((max(n_head, 2), 8, width), F32),
-            pltpu.VMEM(flat, BF16),
-            pltpu.VMEM(flat, BF16),
-            pltpu.VMEM(flat, BF16),
-            dma((4,)),
-            dma((3,)),
+            pltpu.VMEM((ROW, 2, width), F32),
+            pltpu.VMEM((n_rows, 2, width), F32),
+            pltpu.VMEM((max(n_head, 2), 2, width), F32),
+            dma((7,)),
             dma,
             dma,
             dma((2,)),
@@ -562,6 +632,8 @@
             dma((2,)),
             dma((3,)),
             dma((3,)),
+            pltpu.SemaphoreType.REGULAR,
+            pltpu.SemaphoreType.REGULAR,
         ],
         compiler_params=pltpu.CompilerParams(collective_id=0, has_side_effects=True),
     )(
@@ -573,8 +645,22 @@
         values.reshape(flat),
         cotangent.reshape(flat),
     )
+    att, qg, vg, thr_grad, gain_grad = pl.pallas_call(
+        put_out,
+        out_shape=[jax.ShapeDtypeStruct(flat, BF16)] * 3 + [jax.ShapeDtypeStruct((1, width), F32)] * 2,
+        in_specs=[hbm] * 4,
+        out_specs=[hbm] * 5,
+        scratch_shapes=[dma((5,))],
+        compiler_params=pltpu.CompilerParams(vmem_limit_bytes=1 << 20),
+    )(*results)
     whole = (length, heads, width)
-    return att.reshape(whole), qg.reshape(whole), vg.reshape(whole), grads[0], grads[1]
+    return (
+        att.reshape(whole),
+        qg.reshape(whole),
+        vg.reshape(whole),
+        thr_grad.reshape(width),
+        gain_grad.reshape(width),
+    )
 
 
 def solution(mesh):

time: 62.9 us -> 51.6 us (0.82)
  Pallas kernels: 57.2 us -> 50.8 us
  local copies, waits for them, and re-layouts: 4.56 us -> 0 us
    pallas_call x1 -> x2, Pallas kernels: 57.2 us -> 50.8 us  [the longest x1 50 us: on_device(): pl.pallas_call(functools.partial(kernel, dims), out_shape=[pltpu.VMEM(fla...]
    unnamed x7 -> x0, local copies, waits for them, and re-layouts: 3.29 us -> none
    squeeze x1 -> x0, local copies, waits for them, and re-layouts: 1.27 us -> none  [on_device(): grads[1]]
where the time goes in v2:
time: 51.6 us; the launch traced here: 51.4 us
  Pallas kernels  50.8 us (98%)
  between operations  0.64 us (1%)
    pallas_call x1, Pallas kernels, on_device(): pl.pallas_call(functools.partial(kernel, dims), out_shape=[pltpu.VMEM(fla...  50 us

profile of v2, /device:TPU:1, one launch (start us, length us, event | category | flops | bytes accessed | tf_op | source)
XLA Modules:
  0.0 51.4 jit_solution(12638943978398464522)
XLA Ops:
  0.6 50.0 %shard_map.110 = (bf16[512,128]{1,0:T(8,128)(2,1)S(1)}, bf16[512,128]{1,0:T(8,128)(2,1)S(1)}, bf16[512,128]{1,0:T(8,128)(2,1)S(1)}, f32[2,128]{1,0:T(2,128)S(1)}) custom-call(s32[1,256]{1,0:T(1,128)} %bitcast.16, f32[1,128]{1,0:T(1,128)} %bitcast.17, f32[1,128]{1,0:T(1,128)} %bitcast.18, bf16[512,128]{1,0:T(8,128)(2,1)} %bitcast.13, s32[512,128]{1,0:T(8,128)} %bitcast.12, ...), custom_call_target="tpu_custom_call" | custom-call | tf_op jit(solution)/shard_map/pallas_call | solution.py:588
  50.6 0.8 %shard_map.111 = (bf16[512,128]{1,0:T(8,128)(2,1)}, bf16[512,128]{1,0:T(8,128)(2,1)}, bf16[512,128]{1,0:T(8,128)(2,1)}, f32[1,128]{1,0:T(1,128)}, f32[1,128]{1,0:T(1,128)}) custom-call(bf16[512,128]{1,0:T(8,128)(2,1)S(1)} %get-tuple-element.14.att, bf16[512,128]{1,0:T(8,128)(2,1)S(1)} %get-tuple-element.15.qg, bf16[512,128]{1,0:T(8,128)(2,1)S(1)} %get-tuple-element.16.vg, ...), custom_call_target="tpu_custom_call" | custom-call | tf_op jit(solution)/shard_map/pallas_call | solution.py:648

commit v3 on v2

--- a/solution.py
+++ b/solution.py
@@ -48,6 +48,14 @@
     kb,
     vb,
     gb,
+    qf1,
+    cot_h,
+    up_h,
+    spk_h,
+    att_h,
+    ptail,
+    chip_f,
+    land,
     scores,
     dscores,
     base,
@@ -85,6 +93,8 @@
     ar_r,
     token,
     hello,
+    swap_s,
+    swap_r,
 ):
     n_ctx, n_head, row_n, length, heads, width = dims
     chips = row_n // 2
@@ -107,6 +117,9 @@
     def in_row(p):
         return {"ctx": row0 + p}
 
+    def row_peer(k):
+        return in_row(lax.rem(pos + k, row_n))
+
     def to_row(r):
         return {"ctx": r * row_n + pos}
 
@@ -198,14 +211,19 @@
         return c
 
     lax.fori_loop(0, chips - 1, send_meta, 0)
-    pltpu.make_async_remote_copy(
-        src_ref=meta_my,
-        dst_ref=meta.at[pos],
-        send_sem=meta_s,
-        recv_sem=meta_r,
-        device_id=in_row(my_chip * 2 + 1 - my_core),
-        device_id_type=MESH,
-    ).start()
+
+    def to_partner(src, dst, i):
+        return pltpu.make_async_remote_copy(
+            src_ref=src,
+            dst_ref=dst,
+            send_sem=swap_s.at[i],
+            recv_sem=swap_r.at[i],
+            device_id=in_row(my_chip * 2 + 1 - my_core),
+            device_id_type=MESH,
+        )
+
+    own_ends = to_partner(meta_my, meta.at[pos], 2)
+    own_ends.start()
 
     def scatter(h, tail, recv, way):
         def piece(chip):
@@ -333,7 +351,44 @@
         vb[h] = vals
         tail_f[pl.ds(h * width, width), :] = mm((spk * last_f).astype(BF16), vals, 0, 0)
         kb[h] = (spk * thr).astype(BF16)
-        scatter(h, tail_f, recv_f, 0)
+
+    mine = pl.ds(pl.multiple_of(my_core * width, width), width)
+    theirs = pl.ds(pl.multiple_of((1 - my_core) * width, width), width)
+    for_theirs = to_partner(tail_f.at[theirs], ptail.at[theirs], 0)
+    for_theirs.start()
+    own_sums = to_partner(tail_f.at[mine], ptail.at[mine], 3)
+    own_sums.start()
+    own_ends.wait_recv()
+    other = meta[pl.ds(my_chip * 2 + 1 - my_core, 1)].reshape(2, width)
+    same_end = (other[1:2, :] == tail_doc).astype(F32)
+    second = (my_core == 1).astype(F32)
+    own_part = same_end + second * (1.0 - same_end)
+    their_part = 1.0 + second * (same_end - 1.0)
+    for_theirs.wait_recv()
+    chip_f[...] = own_part * tail_f[mine, :] + their_part * ptail[mine, :]
+
+    def chip_piece(t, c):
+        chip = peer_chip(t)
+        pltpu.make_async_remote_copy(
+            src_ref=chip_f.at[pl.ds(chip * pr, pr)],
+            dst_ref=recv_f.at[my_chip],
+            send_sem=st1_s.at[0],
+            recv_sem=st1_r.at[0],
+            device_id=in_row(chip * 2 + my_core),
+            device_id_type=MESH,
+        ).start()
+        return c
+
+    lax.fori_loop(0, chips - 1, chip_piece, 0)
+    recv_f[pl.ds(my_chip, 1)] = chip_f[pl.ds(my_chip * pr, pr), :].reshape(1, pr, width)
+    pieces_f = pltpu.make_async_remote_copy(
+        src_ref=recv_f.at[pl.ds(0, chips - 1)],
+        dst_ref=recv_f.at[pl.ds(0, chips - 1)],
+        send_sem=st1_s.at[0],
+        recv_sem=st1_r.at[0],
+        device_id=row_peer(1),
+        device_id_type=MESH,
+    )
 
     for cp in ins[4:]:
         cp.wait()
@@ -348,39 +403,70 @@
         lane = pl.ds(h, length, stride=heads)
         qf = q_st[lane, :]
         qb[h] = qf.astype(BF16)
+        qf1[h] = (qf * first_f).astype(BF16)
+        cot = cot_st[lane, :]
+        cot_h[h] = cot
+        up_h[h] = cot * gain
+        spk_h[h] = spk_in[lane, :].astype(F32)
         sc = (mm(qb[h], kb[h], 1, 1) * mask[...]).astype(BF16)
         scores[h] = sc
         base[h] = qf + mm(sc, vb[h], 1, 0)
 
     pltpu.make_async_remote_copy(
-        src_ref=meta.at[pl.ds(0, row_n - 1)],
-        dst_ref=meta.at[pl.ds(0, row_n - 1)],
+        src_ref=meta.at[pl.ds(0, row_n - 2)],
+        dst_ref=meta.at[pl.ds(0, row_n - 2)],
         send_sem=meta_s,
         recv_sem=meta_r,
         device_id=in_row(lax.rem(pos + 1, row_n)),
         device_id_type=MESH,
     ).wait_recv()
-    scatter_descriptor(recv_f, 0).wait_recv()
+    pieces_f.wait_recv()
+    row_end = meta[row_n - 1, 1:2, :]
+    run = recv_f[chips - 1]
+    for j in range(chips - 1):
+        run = run + jnp.where(meta[2 * j + 1, 1:2, :] == row_end, recv_f[j], 0.0)
+    zs_f[...] = with_mark(run, row_end)
+    hops_f = [row_hop(k, zs_f, zr_f, 0) for k in (1, 2)]
+    hops_start(hops_f)
     run = recv_f[0]
-    before = meta[0, 1:2, :]
+    before = meta[1, 1:2, :]
     send_f[0] = jnp.zeros((pr, width), F32)
-    for j in range(1, row_n):
-        head_j, tail_j = meta[j, 0:1, :], meta[j, 1:2, :]
+    for j in range(1, chips):
+        head_j, tail_j = meta[2 * j, 0:1, :], meta[2 * j + 1, 1:2, :]
         send_f[j] = jnp.where(before == head_j, run, 0.0)
         run = recv_f[j] + jnp.where(before == tail_j, run, 0.0)
         before = tail_j
-    zs_f[...] = with_mark(run, before)
-    hops_f = [row_hop(k, zs_f, zr_f, 0) for k in (1, 2)]
-    hops_start(hops_f)
     hops_wait_recv(hops_f)
     z1, z2 = zr_f[0, 0:pr, :], zr_f[1, 0:pr, :]
     m1, m2 = zr_f[0, pr : pr + 1, :], zr_f[1, pr : pr + 1, :]
-    for j in range(row_n):
-        head_j = meta[j, 0:1, :]
+    for j in range(chips):
+        head_j = meta[2 * j, 0:1, :]
         send_f[j] = (
             send_f[j] + jnp.where(m1 == head_j, z1, 0.0) + jnp.where(m2 == head_j, z2, 0.0)
         )
-    gather(send_f, carr, 0)
+
+    def enter_chip(t, c):
+        chip = peer_chip(t)
+        pltpu.make_async_remote_copy(
+            src_ref=send_f.at[chip],
+            dst_ref=land.at[my_core, pl.ds(my_chip * pr, pr)],
+            send_sem=st3_s.at[0],
+            recv_sem=st3_r.at[0, 0],
+            device_id=in_row(chip * 2 + my_core),
+            device_id_type=MESH,
+        ).start()
+        return c
+
+    lax.fori_loop(0, chips - 1, enter_chip, 0)
+    land[pl.ds(my_core, 1), pl.ds(my_chip * pr, pr), :] = send_f[pl.ds(my_chip, 1)]
+    entered = pltpu.make_async_remote_copy(
+        src_ref=send_f.at[pl.ds(0, chips - 1)],
+        dst_ref=send_f.at[pl.ds(0, chips - 1)],
+        send_sem=st3_s.at[0],
+        recv_sem=st3_r.at[0, 0],
+        device_id=row_peer(1),
+        device_id_type=MESH,
+    )
 
     @pl.when(my_row > 0)
     def _():
@@ -396,26 +482,42 @@
 
     lax.fori_loop(0, my_row, greet_below, 0)
 
+    own_sums.wait_recv()
+    joins = (other[1:2, :] == head_doc).astype(F32)
+    whole = (other[0:1, :] == other[1:2, :]).astype(F32)
+    by_partner = joins * second
+    by_entry = 1.0 + second * (joins * whole - 1.0)
+
     gain_term = jnp.zeros((1, width), F32)
     cross = jnp.zeros((1, width), F32)
-    for h in range(heads):
-        gather_wait_chips(carr, 0, h)
-        if h == 0:
-            gather_wait_partner(carr, 0)
-        lane = pl.ds(h, length, stride=heads)
-        state = (carr[pl.ds(h * width, width), :] * thr_col).astype(BF16)
-        mixed = base[h] + first_f * mm(qb[h], state, 1, 0)
+    entered.wait_recv()
+    swap = to_partner(land.at[my_core], land.at[my_core], 1)
+    swap.start()
+    for turn in range(2):
+        h = my_core if turn == 0 else 1 - my_core
+        rows = pl.ds(pl.multiple_of(h * width, width), width)
+        if turn == 1:
+            swap.wait_recv()
+        cs = by_entry * land[h] + by_partner * ptail[rows, :]
+        carr[rows, :] = cs
+        state = (cs * thr_col).astype(BF16)
+        mixed = base[h] + mm(qf1[h], state, 1, 0)
         ratio = lax.rsqrt(jnp.mean(mixed * mixed, axis=-1, keepdims=True) + 1e-06)
         normed = mixed * ratio
-        cot = cot_st[lane, :]
-        upstream = cot * gain
+        upstream = up_h[h]
         g = (
             ratio * upstream - normed * (ratio * jnp.mean(normed * upstream, axis=-1, keepdims=True))
         ).astype(BF16)
         gb[h] = g
-        tail_b[pl.ds(h * width, width), :] = mm((q_st[lane, :] * first_f).astype(BF16), g, 0, 0)
-        att_st[lane, :] = normed * gain
-        gain_term = gain_term + jnp.sum(cot * normed, axis=0, keepdims=True)
+        tail = mm(qf1[h], g, 0, 0)
+        tail_b[rows, :] = tail
+        cross = cross + jnp.sum(jnp.transpose(tail * cs), axis=0, keepdims=True)
+        ds = (mm(g, vb[h], 1, 1) * mask[...]).astype(BF16)
+        dscores[h] = ds
+        kg = mm(ds, qb[h], 0, 0)
+        cross = cross + jnp.sum(spk_h[h] * kg, axis=0, keepdims=True)
+        gain_term = gain_term + jnp.sum(cot_h[h] * normed, axis=0, keepdims=True)
+        att_h[h] = normed * gain
 
     def total_copy(buf, mine, stage, device):
         return pltpu.make_async_remote_copy(
@@ -430,11 +532,12 @@
     def total_start(buf, count, mine, stage, device, value):
         buf[pl.ds(mine, 1)] = value.reshape(1, 2, width)
 
-        def body(k, c):
+        def body(t, c):
+            k = count // 2 + ((t + 1) // 2) * (1 - 2 * (t - 2 * (t // 2)))
             total_copy(buf, mine, stage, device(k)).start()
             return c
 
-        lax.fori_loop(1, count, body, 0)
+        lax.fori_loop(0, count - 1, body, 0)
 
     def total_descriptor(buf, count, stage, device):
         part = buf.at[pl.ds(0, count - 1)]
@@ -447,33 +550,21 @@
             device_id_type=MESH,
         )
 
-    def row_peer(k):
-        return in_row(lax.rem(pos + k, row_n))
+    total_start(ar_x, row_n, pos, 0, row_peer, jnp.concatenate([cross, gain_term], axis=0))
+
+    for h in range(heads):
+        scatter(h, tail_b, recv_b, 1)
 
     for h in range(heads):
         lane = pl.ds(h, length, stride=heads)
-        rows = pl.ds(h * width, width)
-        cross = cross + jnp.sum(
-            jnp.transpose(tail_b[rows, :] * carr[rows, :]), axis=0, keepdims=True
-        )
-        ds = (mm(gb[h], vb[h], 1, 1) * mask[...]).astype(BF16)
-        dscores[h] = ds
-        kg = mm(ds, qb[h], 0, 0)
-        cross = cross + jnp.sum(spk_in[lane, :].astype(F32) * kg, axis=0, keepdims=True)
-    total_start(ar_x, row_n, pos, 0, row_peer, jnp.concatenate([cross, gain_term], axis=0))
-
-    for h in range(heads):
-        scatter(h, tail_b, recv_b, 1)
-
-    att_ref[...] = att_st[...].astype(BF16)
-    for h in range(heads):
-        lane = pl.ds(h, length, stride=heads)
+        att_st[lane, :] = att_h[h]
         state = (carr[pl.ds(h * width, width), :] * thr_col).astype(BF16)
         g = gb[h]
         out_st[lane, :] = (
             g.astype(F32) + mm(dscores[h], kb[h], 1, 0) + first_f * mm(g, state, 1, 1)
         )
         vgrad[h] = mm(scores[h], g, 0, 0)
+    att_ref[...] = att_st[...].astype(BF16)
     qg_ref[...] = out_st[...].astype(BF16)
 
     total_descriptor(ar_x, row_n, 0, row_peer).wait_recv()
@@ -528,23 +619,28 @@
     grads_ref[...] = jnp.sum(ar_z[...], axis=0) * scale
 
     pltpu.make_async_remote_copy(
-        src_ref=meta.at[pl.ds(0, row_n - 1)],
-        dst_ref=meta.at[pl.ds(0, row_n - 1)],
+        src_ref=meta.at[pl.ds(0, row_n - 2)],
+        dst_ref=meta.at[pl.ds(0, row_n - 2)],
         send_sem=meta_s,
         recv_sem=meta_r,
         device_id=row_peer(1),
         device_id_type=MESH,
     ).wait_send()
-    for way, recv, send in ((0, recv_f, send_f), (1, recv_b, send_b)):
-        scatter_descriptor(recv, way).wait_send()
-        pltpu.make_async_remote_copy(
-            src_ref=send.at[pl.ds(0, row_n - 1)],
-            dst_ref=send.at[pl.ds(0, row_n - 1)],
-            send_sem=st3_s.at[way],
-            recv_sem=st3_r.at[way, 0],
-            device_id=row_peer(1),
-            device_id_type=MESH,
-        ).wait_send()
+    pieces_f.wait_send()
+    for_theirs.wait_send()
+    own_ends.wait_send()
+    scatter_descriptor(recv_b, 1).wait_send()
+    own_sums.wait_send()
+    entered.wait_send()
+    swap.wait_send()
+    pltpu.make_async_remote_copy(
+        src_ref=send_b.at[pl.ds(0, row_n - 1)],
+        dst_ref=send_b.at[pl.ds(0, row_n - 1)],
+        send_sem=st3_s.at[1],
+        recv_sem=st3_r.at[1, 0],
+        device_id=row_peer(1),
+        device_id_type=MESH,
+    ).wait_send()
     hops_wait_send(hops_f + hops_b)
     total_descriptor(ar_x, row_n, 0, row_peer).wait_send()
     total_descriptor(ar_z, n_rows, 2, along_z).wait_send()
@@ -607,6 +703,14 @@
             pltpu.VMEM((heads, length, width), BF16),
             pltpu.VMEM((heads, length, width), BF16),
             pltpu.VMEM((heads, length, width), BF16),
+            pltpu.VMEM((heads, length, width), BF16),
+            pltpu.VMEM((heads, length, width), F32),
+            pltpu.VMEM((heads, length, width), F32),
+            pltpu.VMEM((heads, length, width), F32),
+            pltpu.VMEM((heads, length, width), F32),
+            pltpu.VMEM(state, F32),
+            pltpu.VMEM((width, width), F32),
+            pltpu.VMEM((heads, width, width), F32),
             pltpu.VMEM((heads, length, length), BF16),
             pltpu.VMEM((heads, length, length), BF16),
             pltpu.VMEM((heads, length, width), F32),
@@ -634,6 +738,8 @@
             dma((3,)),
             pltpu.SemaphoreType.REGULAR,
             pltpu.SemaphoreType.REGULAR,
+            dma((4,)),
+            dma((4,)),
         ],
         compiler_params=pltpu.CompilerParams(collective_id=0, has_side_effects=True),
     )(

time: 51.6 us -> 50.8 us (0.984)
  Pallas kernels: 50.8 us -> 50 us
    pallas_call x1, Pallas kernels: 50 us -> 49.2 us  [on_device(): pl.pallas_call(functools.partial(kernel, dims), out_shape=[pltpu.VMEM(fla...]
where the time goes in v3:
time: 50.8 us; the launch traced here: 50.7 us
  Pallas kernels  50 us (98%)
  between operations  0.64 us (1%)
    pallas_call x1, Pallas kernels, on_device(): pl.pallas_call(functools.partial(kernel, dims), out_shape=[pltpu.VMEM(fla...  49.2 us

profile of v3, /device:TPU:1, one launch (start us, length us, event | category | flops | bytes accessed | tf_op | source)
XLA Modules:
  0.0 50.7 jit_solution(10541867466398791730)
XLA Ops:
  0.6 49.2 %shard_map.110 = (bf16[512,128]{1,0:T(8,128)(2,1)S(1)}, bf16[512,128]{1,0:T(8,128)(2,1)S(1)}, bf16[512,128]{1,0:T(8,128)(2,1)S(1)}, f32[2,128]{1,0:T(2,128)S(1)}) custom-call(s32[1,256]{1,0:T(1,128)} %bitcast.16, f32[1,128]{1,0:T(1,128)} %bitcast.17, f32[1,128]{1,0:T(1,128)} %bitcast.18, bf16[512,128]{1,0:T(8,128)(2,1)} %bitcast.13, s32[512,128]{1,0:T(8,128)} %bitcast.12, ...), custom_call_target="tpu_custom_call" | custom-call | tf_op jit(solution)/shard_map/pallas_call | solution.py:684
  49.9 0.8 %shard_map.111 = (bf16[512,128]{1,0:T(8,128)(2,1)}, bf16[512,128]{1,0:T(8,128)(2,1)}, bf16[512,128]{1,0:T(8,128)(2,1)}, f32[1,128]{1,0:T(1,128)}, f32[1,128]{1,0:T(1,128)}) custom-call(bf16[512,128]{1,0:T(8,128)(2,1)S(1)} %get-tuple-element.14.att, bf16[512,128]{1,0:T(8,128)(2,1)S(1)} %get-tuple-element.15.qg, bf16[512,128]{1,0:T(8,128)(2,1)S(1)} %get-tuple-element.16.vg, ...), custom_call_target="tpu_custom_call" | custom-call | tf_op jit(solution)/shard_map/pallas_call | solution.py:754

commit v4 on v3

--- a/solution.py
+++ b/solution.py
@@ -51,13 +51,14 @@
     qf1,
     cot_h,
     up_h,
-    spk_h,
+    q_h,
+    back_h,
+    sb,
     att_h,
     ptail,
     chip_f,
     land,
     scores,
-    dscores,
     base,
     vgrad,
     meta_my,
@@ -67,7 +68,6 @@
     send_f,
     zs_f,
     zr_f,
-    carr,
     tail_b,
     recv_b,
     send_b,
@@ -350,6 +350,7 @@
         vals = v_st[lane, :].astype(BF16)
         vb[h] = vals
         tail_f[pl.ds(h * width, width), :] = mm((spk * last_f).astype(BF16), vals, 0, 0)
+        sb[h] = spk.astype(BF16)
         kb[h] = (spk * thr).astype(BF16)
 
     mine = pl.ds(pl.multiple_of(my_core * width, width), width)
@@ -407,7 +408,7 @@
         cot = cot_st[lane, :]
         cot_h[h] = cot
         up_h[h] = cot * gain
-        spk_h[h] = spk_in[lane, :].astype(F32)
+        q_h[h] = qf
         sc = (mm(qb[h], kb[h], 1, 1) * mask[...]).astype(BF16)
         scores[h] = sc
         base[h] = qf + mm(sc, vb[h], 1, 0)
@@ -499,23 +500,18 @@
         if turn == 1:
             swap.wait_recv()
         cs = by_entry * land[h] + by_partner * ptail[rows, :]
-        carr[rows, :] = cs
-        state = (cs * thr_col).astype(BF16)
-        mixed = base[h] + mm(qf1[h], state, 1, 0)
-        ratio = lax.rsqrt(jnp.mean(mixed * mixed, axis=-1, keepdims=True) + 1e-06)
+        mixed = base[h] + mm(qf1[h], (cs * thr_col).astype(BF16), 1, 0)
+        upstream = up_h[h]
+        power = jnp.mean(mixed * mixed, axis=-1, keepdims=True)
+        along = jnp.mean(mixed * upstream, axis=-1, keepdims=True)
+        ratio = lax.rsqrt(power + 1e-06)
         normed = mixed * ratio
-        upstream = up_h[h]
-        g = (
-            ratio * upstream - normed * (ratio * jnp.mean(normed * upstream, axis=-1, keepdims=True))
-        ).astype(BF16)
+        g = (ratio * upstream - normed * (ratio * (ratio * along))).astype(BF16)
         gb[h] = g
-        tail = mm(qf1[h], g, 0, 0)
-        tail_b[rows, :] = tail
-        cross = cross + jnp.sum(jnp.transpose(tail * cs), axis=0, keepdims=True)
         ds = (mm(g, vb[h], 1, 1) * mask[...]).astype(BF16)
-        dscores[h] = ds
-        kg = mm(ds, qb[h], 0, 0)
-        cross = cross + jnp.sum(spk_h[h] * kg, axis=0, keepdims=True)
+        back = mm(ds, sb[h], 1, 0) + first_f * mm(g, cs.astype(BF16), 1, 1)
+        back_h[h] = back
+        cross = cross + jnp.sum(q_h[h] * back, axis=0, keepdims=True)
         gain_term = gain_term + jnp.sum(cot_h[h] * normed, axis=0, keepdims=True)
         att_h[h] = normed * gain
 
@@ -553,16 +549,14 @@
     total_start(ar_x, row_n, pos, 0, row_peer, jnp.concatenate([cross, gain_term], axis=0))
 
     for h in range(heads):
+        tail_b[pl.ds(h * width, width), :] = mm(qf1[h], gb[h], 0, 0)
         scatter(h, tail_b, recv_b, 1)
 
     for h in range(heads):
         lane = pl.ds(h, length, stride=heads)
         att_st[lane, :] = att_h[h]
-        state = (carr[pl.ds(h * width, width), :] * thr_col).astype(BF16)
         g = gb[h]
-        out_st[lane, :] = (
-            g.astype(F32) + mm(dscores[h], kb[h], 1, 0) + first_f * mm(g, state, 1, 1)
-        )
+        out_st[lane, :] = g.astype(F32) + thr * back_h[h]
         vgrad[h] = mm(scores[h], g, 0, 0)
     att_ref[...] = att_st[...].astype(BF16)
     qg_ref[...] = out_st[...].astype(BF16)
@@ -708,16 +702,17 @@
             pltpu.VMEM((heads, length, width), F32),
             pltpu.VMEM((heads, length, width), F32),
             pltpu.VMEM((heads, length, width), F32),
+            pltpu.VMEM((heads, length, width), BF16),
+            pltpu.VMEM((heads, length, width), F32),
             pltpu.VMEM(state, F32),
             pltpu.VMEM((width, width), F32),
             pltpu.VMEM((heads, width, width), F32),
-            pltpu.VMEM((heads, length, length), BF16),
             pltpu.VMEM((heads, length, length), BF16),
             pltpu.VMEM((heads, length, width), F32),
             pltpu.VMEM((heads, length, width), F32),
             pltpu.VMEM((2, width), F32),
             pltpu.VMEM((ROW, 2, width), F32),
-            *one_way,
+            *one_way[:-1],
             *one_way,
             pltpu.VMEM(flat, F32),
             pltpu.VMEM(flat, F32),

time: 50.8 us -> 50.4 us (level)
  no operation moved by 1% of the time
where the time goes in v4:
time: 50.4 us; the launch traced here: 50.3 us
  Pallas kernels  49.6 us (98%)
  between operations  0.64 us (1%)
    pallas_call x1, Pallas kernels, on_device(): pl.pallas_call(functools.partial(kernel, dims), out_shape=[pltpu.VMEM(fla...  48.9 us

profile of v4, /device:TPU:1, one launch (start us, length us, event | category | flops | bytes accessed | tf_op | source)
XLA Modules:
  0.0 50.3 jit_solution(16561054876317870532)
XLA Ops:
  0.6 48.9 %shard_map.110 = (bf16[512,128]{1,0:T(8,128)(2,1)S(1)}, bf16[512,128]{1,0:T(8,128)(2,1)S(1)}, bf16[512,128]{1,0:T(8,128)(2,1)S(1)}, f32[2,128]{1,0:T(2,128)S(1)}) custom-call(s32[1,256]{1,0:T(1,128)} %bitcast.16, f32[1,128]{1,0:T(1,128)} %bitcast.17, f32[1,128]{1,0:T(1,128)} %bitcast.18, bf16[512,128]{1,0:T(8,128)(2,1)} %bitcast.13, s32[512,128]{1,0:T(8,128)} %bitcast.12, ...), custom_call_target="tpu_custom_call" | custom-call | tf_op jit(solution)/shard_map/pallas_call | solution.py:678
  49.5 0.8 %shard_map.111 = (bf16[512,128]{1,0:T(8,128)(2,1)}, bf16[512,128]{1,0:T(8,128)(2,1)}, bf16[512,128]{1,0:T(8,128)(2,1)}, f32[1,128]{1,0:T(1,128)}, f32[1,128]{1,0:T(1,128)}) custom-call(bf16[512,128]{1,0:T(8,128)(2,1)S(1)} %get-tuple-element.14.att, bf16[512,128]{1,0:T(8,128)(2,1)S(1)} %get-tuple-element.15.qg, bf16[512,128]{1,0:T(8,128)(2,1)S(1)} %get-tuple-element.16.vg, ...), custom_call_target="tpu_custom_call" | custom-call | tf_op jit(solution)/shard_map/pallas_call | solution.py:749

commit v5 on v4

--- a/solution.py
+++ b/solution.py
@@ -143,7 +143,7 @@
             )
         )
     ]
-    for cp in ins:
+    for cp in ins[:4]:
         cp.start()
 
     barrier = pltpu.get_barrier_semaphore()
@@ -339,6 +339,8 @@
     def with_mark(total, mark):
         return jnp.concatenate([total, jnp.broadcast_to(mark, (8, width))], axis=0)
 
+    for cp in ins[4:]:
+        cp.start()
     ins[2].wait()
     ins[3].wait()
     v_st[...] = v_in[...].astype(F32)
@@ -643,13 +645,12 @@
 
 
 def put_out(att, qg, vg, grads, att_hbm, qg_hbm, vg_hbm, thr_hbm, gain_hbm, sem):
-    pairs = (
-        (att, att_hbm),
-        (qg, qg_hbm),
-        (vg, vg_hbm),
-        (grads.at[pl.ds(0, 1)], thr_hbm),
-        (grads.at[pl.ds(1, 1)], gain_hbm),
-    )
+    pairs = [(grads.at[pl.ds(0, 1)], thr_hbm), (grads.at[pl.ds(1, 1)], gain_hbm)]
+    half = att.shape[0] // 2
+    for src, dst in ((att, att_hbm), (qg, qg_hbm), (vg, vg_hbm)):
+        for part in range(2):
+            rows = pl.ds(part * half, half)
+            pairs.append((src.at[rows], dst.at[rows]))
     copies = [pltpu.make_async_copy(src, dst, sem.at[i]) for i, (src, dst) in enumerate(pairs)]
     for copy in copies:
         copy.start()
@@ -751,7 +752,7 @@
         out_shape=[jax.ShapeDtypeStruct(flat, BF16)] * 3 + [jax.ShapeDtypeStruct((1, width), F32)] * 2,
         in_specs=[hbm] * 4,
         out_specs=[hbm] * 5,
-        scratch_shapes=[dma((5,))],
+        scratch_shapes=[dma((8,))],
         compiler_params=pltpu.CompilerParams(vmem_limit_bytes=1 << 20),
     )(*results)
     whole = (length, heads, width)

time: 50.4 us -> 50.5 us (level)
  no operation moved by 1% of the time
where the time goes in v5:
time: 50.5 us; the launch traced here: 50.3 us
  Pallas kernels  49.7 us (98%)
  between operations  0.64 us (1%)
    pallas_call x1, Pallas kernels, on_device(): pl.pallas_call(functools.partial(kernel, dims), out_shape=[pltpu.VMEM(fla...  48.8 us

profile of v5, /device:TPU:1, one launch (start us, length us, event | category | flops | bytes accessed | tf_op | source)
XLA Modules:
  0.0 50.3 jit_solution(17816776495659589746)
XLA Ops:
  0.6 48.8 %shard_map.110 = (bf16[512,128]{1,0:T(8,128)(2,1)S(1)}, bf16[512,128]{1,0:T(8,128)(2,1)S(1)}, bf16[512,128]{1,0:T(8,128)(2,1)S(1)}, f32[2,128]{1,0:T(2,128)S(1)}) custom-call(s32[1,256]{1,0:T(1,128)} %bitcast.16, f32[1,128]{1,0:T(1,128)} %bitcast.17, f32[1,128]{1,0:T(1,128)} %bitcast.18, bf16[512,128]{1,0:T(8,128)(2,1)} %bitcast.13, s32[512,128]{1,0:T(8,128)} %bitcast.12, ...), custom_call_target="tpu_custom_call" | custom-call | tf_op jit(solution)/shard_map/pallas_call | solution.py:679
  49.5 0.8 %shard_map.111 = (bf16[512,128]{1,0:T(8,128)(2,1)}, bf16[512,128]{1,0:T(8,128)(2,1)}, bf16[512,128]{1,0:T(8,128)(2,1)}, f32[1,128]{1,0:T(1,128)}, f32[1,128]{1,0:T(1,128)}) custom-call(bf16[512,128]{1,0:T(8,128)(2,1)S(1)} %get-tuple-element.14.att, bf16[512,128]{1,0:T(8,128)(2,1)S(1)} %get-tuple-element.15.qg, bf16[512,128]{1,0:T(8,128)(2,1)S(1)} %get-tuple-element.16.vg, ...), custom_call_target="tpu_custom_call" | custom-call | tf_op jit(solution)/shard_map/pallas_call | solution.py:750

commit v6 on v5

--- a/solution.py
+++ b/solution.py
@@ -531,7 +531,8 @@
         buf[pl.ds(mine, 1)] = value.reshape(1, 2, width)
 
         def body(t, c):
-            k = count // 2 + ((t + 1) // 2) * (1 - 2 * (t - 2 * (t // 2)))
+            far_first = count // 2 + ((t + 1) // 2) * (1 - 2 * (t - 2 * (t // 2)))
+            k = t + 1 if stage == 2 else far_first
             total_copy(buf, mine, stage, device(k)).start()
             return c
 

time: 50.5 us -> 50.5 us (level)
  no operation moved by 1% of the time
where the time goes in v6:
time: 50.5 us; the launch traced here: 50.3 us
  Pallas kernels  49.6 us (98%)
  between operations  0.64 us (1%)
    pallas_call x1, Pallas kernels, on_device(): pl.pallas_call(functools.partial(kernel, dims), out_shape=[pltpu.VMEM(fla...  48.8 us

profile of v6, /device:TPU:1, one launch (start us, length us, event | category | flops | bytes accessed | tf_op | source)
XLA Modules:
  0.0 50.3 jit_solution(9553902953536843014)
XLA Ops:
  0.6 48.8 %shard_map.110 = (bf16[512,128]{1,0:T(8,128)(2,1)S(1)}, bf16[512,128]{1,0:T(8,128)(2,1)S(1)}, bf16[512,128]{1,0:T(8,128)(2,1)S(1)}, f32[2,128]{1,0:T(2,128)S(1)}) custom-call(s32[1,256]{1,0:T(1,128)} %bitcast.16, f32[1,128]{1,0:T(1,128)} %bitcast.17, f32[1,128]{1,0:T(1,128)} %bitcast.18, bf16[512,128]{1,0:T(8,128)(2,1)} %bitcast.13, s32[512,128]{1,0:T(8,128)} %bitcast.12, ...), custom_call_target="tpu_custom_call" | custom-call | tf_op jit(solution)/shard_map/pallas_call | solution.py:680
  49.5 0.8 %shard_map.111 = (bf16[512,128]{1,0:T(8,128)(2,1)}, bf16[512,128]{1,0:T(8,128)(2,1)}, bf16[512,128]{1,0:T(8,128)(2,1)}, f32[1,128]{1,0:T(1,128)}, f32[1,128]{1,0:T(1,128)}) custom-call(bf16[512,128]{1,0:T(8,128)(2,1)S(1)} %get-tuple-element.14.att, bf16[512,128]{1,0:T(8,128)(2,1)S(1)} %get-tuple-element.15.qg, bf16[512,128]{1,0:T(8,128)(2,1)S(1)} %get-tuple-element.16.vg, ...), custom_call_target="tpu_custom_call" | custom-call | tf_op jit(solution)/shard_map/pallas_call | solution.py:751
